TPU v7x, 512 devices: a whole 4x8x8 slice. The times are simulated.
512 devices in a mesh: section: 2 (over y_lo), channel: 16 (over x, y_hi), block: 16 (over z, core).
Axes of the slice: x: 4, y: 8 (y_hi: 4, y_lo: 2; y = y_hi * 2 + y_lo), z: 8, core: 2. Of those that a mesh axis runs over, the one named last changes fastest.
Arguments:
- env: bfloat16 [2, 16, 16, 512, 512], P('section', 'channel', 'block'), may hold values from -6 to 6
- site_tensor: bfloat16 [2, 4, 16, 512, 512], P('section', None, 'block'), may hold values from -0.25 to 0.25
- mpo: bfloat16 [2, 16, 16, 4], P('section'), may hold values from -2 to 2
- channel_mask: int32 [2, 16, 16], P('section'), may hold values 0 or 1
- block_mask: int32 [2, 4, 16], P('section', None, 'block'), may hold values 0 or 1
- state_charge: int32 [4], replicated, may hold values from 0 to 1, as said below
- psi: bfloat16 [2, 16, 512, 512], P('section', 'block'), may hold values from -0.0014648438 to 0.0014648438
Outputs:
- new_env: bfloat16 [2, 16, 16, 512, 512], P('section', 'channel', 'block')
- new_psi: bfloat16 [512, 2, 16, 512], P('channel', 'section', 'block')
Inputs may be any that keep to these rules, and one draw needn't show every extreme that they name: `state_charge`: half of the 4 site states carry charge 0, the others charge 1.
All inputs are finite; a program needn't handle non-finite values. No bound on the sum of `channel_mask` or of `block_mask` on one device may be relied on, other than what follows from the above.
Results may differ from a plain program's by a relative error of at most 0.017.
Values may be sent and summed in bfloat16 or wider, within the bound.
A program may use at most 64 MiB of HBM per device.

v0:
```python
import jax
import jax.numpy as jnp
from jax import lax
from jax.sharding import PartitionSpec as P


def padded(block, sides, width):
    for axis, dim in sides:
        count = lax.axis_size(axis)
        forward = [(i, i + 1) for i in range(count - 1)]
        backward = [(target, source) for source, target in forward]
        low = lax.ppermute(
            lax.slice_in_dim(block, block.shape[dim] - width, None, axis=dim), axis, forward
        )
        high = lax.ppermute(lax.slice_in_dim(block, 0, width, axis=dim), axis, backward)
        block = jnp.concatenate([low, block, high], axis=dim)
    return block


def from_partner(value, axis, bit):
    return lax.ppermute(value, axis, [(i, i ^ 1 << bit) for i in range(lax.axis_size(axis))])


def per_device(env, site_tensor, mpo, channel_mask, block_mask, state_charge, psi):
    section = lax.axis_index("section")
    own_env = env[0]
    site_blocks = site_tensor[0]
    weights = mpo[0] * channel_mask[0].astype(jnp.bfloat16)[:, :, None]
    chan_dev = own_env.shape[0]
    offset_w = lax.axis_index("channel") * chan_dev
    gathered = lax.all_gather(own_env, "channel", axis=0, tiled=True)
    local_w = lax.dynamic_slice_in_dim(weights, offset_w, chan_dev, 1)
    blended_environment = jnp.einsum(
        "wvs,wqab->vsqab", local_w, gathered, preferred_element_type=jnp.float32
    ).astype(jnp.bfloat16)
    product = jnp.einsum(
        "vsqac,sqcb->vsqab", blended_environment, site_blocks, preferred_element_type=jnp.float32
    ).astype(jnp.bfloat16)
    contracted_layers = jnp.einsum(
        "sqca,vsqcb->vsqab", site_blocks, product, preferred_element_type=jnp.float32
    )
    charge_label = state_charge.astype(jnp.float32)
    sector_present = block_mask[0].astype(jnp.float32)
    resident_part = jnp.einsum(
        "vsqab,sq->vqab", contracted_layers, sector_present * (1.0 - charge_label)[:, None]
    )
    outgoing_part = jnp.einsum(
        "vsqab,sq->vqab", contracted_layers, sector_present * charge_label[:, None]
    ).astype(jnp.bfloat16)
    rim_cells = padded(outgoing_part, (("block", 1),), 1)
    sector_count = outgoing_part.shape[1]
    shifted = jnp.where(section == 0, rim_cells[:, :sector_count], rim_cells[:, 2:])
    new_env = (resident_part + shifted.astype(jnp.float32)).astype(jnp.bfloat16)
    partner = from_partner(new_env, "section", 0)
    left_env = jnp.where(section == 0, new_env, partner)
    right_env = jnp.where(section == 0, partner, new_env)
    applied = jnp.einsum(
        "wqab,vqbd->wvqad", left_env, psi, preferred_element_type=jnp.float32
    ).astype(jnp.bfloat16)
    summed = lax.psum_scatter(
        jnp.einsum("wvqad,wqcd->avqc", applied, right_env, preferred_element_type=jnp.float32),
        "channel",
        scatter_dimension=0,
        tiled=True,
    )
    return (new_env[None], summed.astype(jnp.bfloat16))


def solution(mesh):
    return jax.shard_map(
        per_device,
        mesh=mesh,
        in_specs=(
            P("section", "channel", "block", None, None),
            P("section", None, "block", None, None),
            P("section", None, None, None),
            P("section", None, None),
            P("section", None, "block"),
            P(),
            P("section", "block", None, None),
        ),
        out_specs=(
            P("section", "channel", "block", None, None),
            P("channel", "section", "block", None),
        ),
        check_vma=False,
    )
```

profile of v0, /device:TPU:338, one launch (start us, length us, event | category | flops | bytes accessed | tf_op | source)
XLA Modules:
  0.0 582.3 jit_solution(246775809543533413)
XLA Ops:
  7.2 0.0 copy-start
  7.2 0.0 all-gather.3.cloned.1.call-start
  7.2 0.7 all-gather.3.cloned.1.call-update
  7.9 0.7 convert_bitcast_fusion
  8.6 0.1 constant_dynamic-slice_fusion
  8.7 0.8 dynamic-slice_multiply_fusion
  9.5 0.1 copy.12
  9.6 123.7 %all-gather.3.cloned.1.call-done = bf16[16,1,1,512,512]{4,3,2,1,0:T(8,128)(2,1)} async-done(((bf16[1,1,1,512,512]{4,3,2,1,0:T(8,128)(2,1)}), bf16[16,1,1,512,512]{4,3,2,1,0:T(8,128)(2,1)}) %all-gather.3.cloned.1.call-update) | async-done | bytes 8388624 | tf_op jit(solution)/shard_map/all_gather | solution.py:31
  133.3 9.8 %fusion = bf16[4,512,512]{2,0,1:T(4,128)(2,1)} fusion(bf16[16,512,512]{2,1,0:T(8,128)(2,1)} %bitcast.85, bf16[16,1,4]{0,2,1:T(4,128)(2,1)S(1)} %copy.12), kind=kOutput, calls=%fused_computation | convolution fusion | flops 33554432 | bytes 10485888 | tf_op jit(solution)/shard_map/wvs,wqab->vsqab/dot_general | solution.py:33
  143.1 0.0 copy-done
  143.1 5.3 convolution_bitcast_fusion
  148.4 0.0 copy-start.2
  148.4 0.0 copy-start.3
  148.4 4.5 copy.19
  152.9 0.0 copy-done.2
  152.9 0.0 copy-done.3
  152.9 2.8 fusion.23
  155.8 0.1 copy.34
  155.9 1.9 collective-permute-start
  157.8 3.6 collective-permute-start.1
  161.5 2.8 fusion.25
  164.3 2.1 collective-permute-done
  166.4 1.8 collective-permute-done.1
  168.1 0.3 fusion.10
  168.4 0.0 copy-start.1
  168.4 3.8 collective-permute-start.2
  172.3 1.3 dynamic-slice
  174.2 10.4 %collective-permute-done.2 = bf16[1,1,512,512]{3,2,1,0:T(8,128)(2,1)S(1)} collective-permute-done((bf16[1,1,512,512]{3,2,1,0:T(8,128)(2,1)S(1)}, bf16[1,1,512,512]{3,2,1,0:T(8,128)(2,1)S(1)}, u32[]{:S(2)}, u32[]{:S(2)}) %collective-permute-start.2) | collective-permute-done | bytes 524320 | tf_op jit(solution)/shard_map/ppermute | solution.py:21
  184.6 0.0 copy-done.1
  184.6 2.8 convolution_bitcast_fusion.1
  187.5 2.4 copy.14
  189.9 384.0 %all-reduce.2 = bf16[512,1,1,512]{3,2,1,0:T(2,128)(2,1)} all-reduce(f32[512,1,1,512]{3,2,1,0:T(1,128)S(1)} %copy.14), channel_id=3, replica_groups=mesh['section'=2,'channel'=16,'block'=16] {'channel'}, use_global_device_ids=true, to_apply=%region_0.1.clone | all-reduce | flops 262144 | bytes 1572864
  573.9 0.9 dynamic-slice_convert_fusion
  574.8 0.6 copy.15
Async XLA Ops:
  7.2 135.9 %copy-start = (bf16[1,4,1,512,512]{4,3,2,1,0:T(8,128)(2,1)S(1)}, bf16[1,4,1,512,512]{4,3,2,1,0:T(8,128)(2,1)}, u32[]{:S(2)}) copy-start(bf16[1,4,1,512,512]{4,3,2,1,0:T(8,128)(2,1)} %param.8) | copy-start | bytes 6291460
  7.2 126.2 %all-gather.3.cloned.1.call-start = ((), (), s32[]{:S(2)}) async-start(), calls=%async_computation | async-start | bytes 8912896 | tf_op jit(solution)/shard_map/all_gather | solution.py:31
  148.4 4.5 copy-start.2
  148.4 4.5 copy-start.3
  155.9 10.5 %collective-permute-start = (bf16[1,1,512,512]{3,2,1,0:T(8,128)(2,1)S(1)}, bf16[1,1,512,512]{3,2,1,0:T(8,128)(2,1)S(1)}, u32[]{:S(2)}, u32[]{:S(2)}) collective-permute-start(bf16[1,1,512,512]{3,2,1,0:T(8,128)(2,1)S(1)} %bitcast.86), channel_id=1, source_target_pairs={{0,1},{1,2},{2,3},{3,4},{4,5},{5,6},{6,7},{7,8},{8,9},{9,10},{10,1... | collective-permute-start | bytes 1572872 | tf_op jit(solution)/shard_map/ppermute | solution.py:12
  157.8 10.3 %collective-permute-start.1 = (bf16[1,1,512,512]{3,2,1,0:T(8,128)(2,1)S(1)}, bf16[1,1,512,512]{3,2,1,0:T(8,128)(2,1)}, u32[]{:S(2)}, u32[]{:S(2)}) collective-permute-start(bf16[1,1,512,512]{3,2,1,0:T(8,128)(2,1)S(1)} %bitcast.87), channel_id=1, source_target_pairs={{1,0},{2,1},{3,2},{4,3},{5,4},{6,5},{7,6},{8,7},{9,8},{10,9},{11,1... | collective-permute-start | bytes 1572872 | tf_op jit(solution)/shard_map/ppermute | solution.py:15
  168.4 16.2 %copy-start.1 = (bf16[1,1,512,512]{3,2,1,0:T(8,128)(2,1)}, bf16[1,1,512,512]{3,2,1,0:T(8,128)(2,1)S(1)}, u32[]{:S(2)}) copy-start(bf16[1,1,512,512]{3,2,1,0:T(8,128)(2,1)S(1)} %fusion.10) | copy-start | bytes 1572868
  168.4 16.2 %collective-permute-start.2 = (bf16[1,1,512,512]{3,2,1,0:T(8,128)(2,1)S(1)}, bf16[1,1,512,512]{3,2,1,0:T(8,128)(2,1)S(1)}, u32[]{:S(2)}, u32[]{:S(2)}) collective-permute-start(bf16[1,1,512,512]{3,2,1,0:T(8,128)(2,1)S(1)} %fusion.10), channel_id=1, source_target_pairs={{0,256},{256,0},{1,257},{257,1},{2,258},{258,2},{3,259},{259,3},{4... | collective-permute-start | bytes 1572872 | tf_op jit(solution)/shard_map/ppermute | solution.py:21
Sparse Core Ops, SparseCore 0:
  11.0 122.2 all-gather.2
where the time goes:
time: 583 us; the launch traced here: 582 us
  blocking collectives  384 us (66%)
  waiting for transfers between devices  139 us (24%)
  matrix products  23.6 us (4%)
  between operations  14.8 us (3%)
  local copies, waits for them, and re-layouts  10 us (2%)
  starting transfers between devices  9.44 us (2%)
    unnamed x1, blocking collectives  384 us
    all_gather x1, waiting for transfers between devices, per_device(): gathered = lax.all_gather(own_env, 'channel', axis=0, tiled=True)  124 us
  transfers between devices with their start and end apart: 4, of which 4 were waited for; matrix products, arithmetic and copies ran while one was open for 1% of the time, Pallas kernels for 0%

commit v1 on v0

v1 whole, which is shorter than its diff:
```python
import functools

import jax
import jax.numpy as jnp
from jax import lax
from jax.experimental import pallas as pl
from jax.experimental.pallas import tpu as pltpu
from jax.sharding import PartitionSpec as P

MESH = pl.DeviceIdType.MESH
F32, BF16 = jnp.float32, jnp.bfloat16
N = 512
NX = 4
NY = 4
NCH = 4
R = 128 // NCH
SUB = R // 16
LAST = (((1,), (1,)), ((), ()))


def mod4(value):
    return lax.rem(value, 4)


def mix_matrix(mpo_ref, cmask_ref, bmask_ref, charge_ref, yh):
    rows = lax.broadcasted_iota(jnp.int32, (256, 16), 0)
    lane = lax.broadcasted_iota(jnp.int32, (256, 16), 1)
    want_v = lax.rem(rows // 16, 4) * 4 + yh
    pick_v = (lane == want_v).astype(F32)
    rows_s = lax.broadcasted_iota(jnp.int32, (256, 4), 0)
    lane_s = lax.broadcasted_iota(jnp.int32, (256, 4), 1)
    slots, _ = state_slots(charge_ref)
    pick_s = jnp.zeros((256, 4), F32)
    for s in range(4):
        hit = (lane_s == s) & (rows_s // 64 == slots[s])
        pick_s = jnp.where(hit, bmask_ref[s].astype(F32), pick_s)
    pick_s = pick_s.astype(BF16)
    cmask = cmask_ref[...].astype(F32).astype(BF16)
    allowed = lax.dot_general(pick_v.astype(BF16), cmask, LAST, preferred_element_type=F32)
    values = jnp.zeros((256, 16), F32)
    for w in range(16):
        coupling = jnp.dot(pick_s, mpo_ref[w], preferred_element_type=F32) * pick_v
        column = jnp.sum(coupling, axis=1, keepdims=True)
        values = jnp.where(lane == w, column, values)
    values = values * allowed
    spread_w = lax.broadcasted_iota(jnp.int32, (16, 256), 0)
    spread_c = lax.broadcasted_iota(jnp.int32, (16, 256), 1) // 16
    spread = (spread_w == lax.rem(spread_c, 4) * 4 + spread_c // 4).astype(BF16)
    full = jnp.dot(values.astype(BF16), spread, preferred_element_type=F32)
    row = lax.broadcasted_iota(jnp.int32, (256, 256), 0)
    col = lax.broadcasted_iota(jnp.int32, (256, 256), 1)
    return jnp.where(lax.rem(row, 16) == lax.rem(col, 16), full, 0.0).astype(BF16)


def state_slots(charge_ref):
    charge = [charge_ref[s] for s in range(4)]
    slots = []
    ones = jnp.int32(0)
    for s in range(4):
        slots.append(jnp.where(charge[s] == 1, 2 + ones, s - ones))
        ones = ones + charge[s]
    order = []
    for k in range(4):
        place = jnp.int32(0)
        for s in range(4):
            place = place + jnp.where(slots[s] == k, s, 0)
        order.append(place)
    return slots, order


def kernel(
    charge_ref, bmask_ref, env_ref, site_ref, mpo_ref, cmask_ref, psi_ref,
    new_env_ref, new_psi_ref,
    site_v, srt, near, psi_v, psi_t, kmat, gath, mixed, sent, prod, turned, acc,
    mine, other, half, zsum, zparts, zrows, ysend, yrecv,
    site_sem, psi_sem, own_sem, out_sem,
    x_send, x_recv, y_send, y_recv, r_send, r_recv, near_send, near_recv,
    p_send, p_recv, n_send, n_recv, z_send, z_recv, f_send, f_recv,
):
    g = lax.axis_index("section")
    c = lax.axis_index("channel")
    q = lax.axis_index("block")
    x, yh = c // 4, lax.rem(c, 4)
    up = lax.rem(q + 1, 16)
    down = lax.rem(q + 15, 16)
    target = jnp.where(g == 0, up, down)
    origin = jnp.where(g == 0, down, up)
    fed = jnp.where(g == 0, q > 0, q < 15)
    at_x = [mod4(x + i) * 4 + yh for i in range(4)]
    at_y = [x * 4 + mod4(yh + i) for i in range(4)]

    def to(channel=None, block=None, section=None):
        where = {}
        if section is not None:
            where["section"] = section
        if channel is not None:
            where["channel"] = channel
        if block is not None:
            where["block"] = block
        return where

    def send(src, dst, send_sem, recv_sem, where):
        pltpu.make_async_remote_copy(
            src_ref=src, dst_ref=dst, send_sem=send_sem, recv_sem=recv_sem, device_id=where, device_id_type=MESH
        ).start()

    def took(ref, sem):
        pltpu.make_async_copy(ref, ref, sem).wait()

    site_in = pltpu.make_async_copy(site_ref, site_v, site_sem)
    site_in.start()
    psi_in = pltpu.make_async_copy(psi_ref, psi_v, psi_sem)
    psi_in.start()
    for j in range(NCH):
        pltpu.make_async_copy(env_ref.at[pl.ds(x * 128 + j * R, R)], gath.at[j, yh * 4 + x], own_sem).start()

    barrier = pltpu.get_barrier_semaphore()
    for i in range(1, 4):
        pl.semaphore_signal(barrier, inc=1, device_id=to(channel=at_x[i]), device_id_type=MESH)
        pl.semaphore_signal(barrier, inc=1, device_id=to(channel=at_y[i]), device_id_type=MESH)
    for i in range(4):
        pl.semaphore_signal(barrier, inc=1, device_id=to(channel=at_x[i], block=origin), device_id_type=MESH)
    pl.semaphore_signal(barrier, inc=1, device_id=to(section=1 - g), device_id_type=MESH)
    pl.semaphore_wait(barrier, 11)

    for j in range(NCH):
        for i in range(1, 4):
            send(
                env_ref.at[pl.ds(mod4(x + i) * 128 + j * R, R)], gath.at[j, yh * 4 + x],
                x_send, x_recv.at[j], to(channel=at_x[i]),
            )

    site_in.wait()
    _, order = state_slots(charge_ref)
    for k in range(4):
        srt[k] = site_v[order[k]]
    send(srt.at[pl.ds(2, 2)], near, near_send, near_recv, to(block=target))

    def pass_on(j):
        took(gath.at[j, pl.ds(0, 3)], x_recv.at[j])
        rows = gath.at[j, pl.ds(yh * 4, 4)]
        send(rows, rows, y_send, y_recv.at[j, 0], to(channel=at_y[1]))
        send(rows, rows, y_send, y_recv.at[j, 1], to(channel=at_y[3]))

    def relay(j):
        before = gath.at[j, pl.ds(mod4(yh + 3) * 4, 2)]
        took(gath.at[j, pl.ds(0, 4)], y_recv.at[j, 0])
        send(before, before, r_send, r_recv.at[j, 0], to(channel=at_y[1]))
        after = gath.at[j, pl.ds(mod4(yh + 1) * 4 + 2, 2)]
        took(gath.at[j, pl.ds(0, 4)], y_recv.at[j, 1])
        send(after, after, r_send, r_recv.at[j, 1], to(channel=at_y[3]))

    def multiply(j):
        took(gath.at[j, pl.ds(0, 2)], r_recv.at[j, 0])
        took(gath.at[j, pl.ds(0, 2)], r_recv.at[j, 1])
        for sub in range(SUB):
            piece = gath[j, :, sub * 16 : sub * 16 + 16, :].reshape(256, N)
            blended = jnp.dot(kmat[...], piece, preferred_element_type=F32)
            mixed[:, sub * 16 : sub * 16 + 16, :] = blended.astype(BF16).reshape(16, 16, N)
        for k in range(4):
            product = jnp.dot(mixed[4 * k : 4 * k + 4].reshape(4 * R, N), srt[k], preferred_element_type=F32)
            product = product.astype(BF16).reshape(4, R, N)
            for vx in range(4):
                sent[j, vx * 4 + k] = product[vx]
        for i in range(1, 4):
            v = mod4(x + i)
            send(sent.at[j, pl.ds(v * 4, 2)], prod.at[j, pl.ds(x * 4, 2)], p_send, p_recv.at[j], to(channel=at_x[i]))
        for i in range(4):
            v = mod4(x + i)
            send(
                sent.at[j, pl.ds(v * 4 + 2, 2)], prod.at[j, pl.ds(x * 4 + 2, 2)],
                p_send, p_recv.at[j], to(channel=at_x[i], block=target),
            )
        prod[j, pl.ds(x * 4, 2)] = sent[j, pl.ds(x * 4, 2)]

    def accumulate(j):
        took(prod.at[j, pl.ds(0, 14)], p_recv.at[j])

        def tile(t, carry):
            rows = pl.ds(pl.multiple_of(t * 128, 128), 128)
            part = jnp.dot(turned[j, rows, :], prod[j].reshape(16 * R, N), preferred_element_type=F32)
            acc[rows, :] = part if j == 0 else acc[rows, :] + part
            return carry

        lax.fori_loop(0, 4, tile, 0)

    def turn(k):
        for j in range(NCH):
            for xs in range(4):
                rows = slice(xs * 128 + j * R, xs * 128 + j * R + R)
                block = srt[k, rows, :] if k < 2 else jnp.where(fed, near[k - 2, rows, :].astype(F32), 0.0).astype(BF16)
                columns = slice((xs * 4 + k) * R, (xs * 4 + k) * R + R)
                turned[j, :, columns] = block.T

    took(gath.at[0:NCH, 0], own_sem)
    pass_on(0)
    pass_on(1)

    kmat[...] = mix_matrix(mpo_ref, cmask_ref, bmask_ref, charge_ref, yh)
    psi_in.wait()

    @pl.when(g == 0)
    def _():
        psi_t[...] = psi_v[...]

    @pl.when(g == 1)
    def _():
        psi_t[...] = psi_v[...].T

    turn(0)
    turn(1)

    for j in range(NCH):
        relay(j)
        if j + 2 < NCH:
            pass_on(j + 2)
        if j == 0:
            took(near, near_recv)
            turn(2)
            turn(3)
        if j >= 1:
            multiply(j - 1)
        if j >= 2:
            accumulate(j - 2)
    multiply(NCH - 1)
    accumulate(NCH - 2)

    final = NCH - 1
    took(prod.at[final, pl.ds(0, 14)], p_recv.at[final])
    starts = [pl.multiple_of(mod4(x + i) * 128, 128) for i in range(4)]
    for i in (1, 2, 3, 0):
        rows = pl.ds(starts[i], 128)
        part = jnp.dot(turned[final, rows, :], prod[final].reshape(16 * R, N), preferred_element_type=F32)
        mine[rows, :] = (acc[rows, :] + part).astype(BF16)
        send(mine.at[rows], other.at[rows], n_send, n_recv.at[i], to(section=1 - g))
    out = pltpu.make_async_copy(mine, new_env_ref, out_sem)
    out.start()
    for i in range(4):
        rows = pl.ds(i * 128, 128)
        half[rows, :] = jnp.dot(mine[rows, :], psi_t[...], preferred_element_type=F32).astype(BF16)

    @pl.when(g == 0)
    def _():
        for i in (1, 2, 3, 0):
            rows = pl.ds(starts[i], 128)
            took(other.at[pl.ds(0, 128)], n_recv.at[i])
            part = lax.dot_general(half[...], other[rows, :], LAST, preferred_element_type=F32)
            zsum[:, rows] = part.astype(BF16)
            for d in range(1, 4):
                send(
                    zsum.at[pl.ds(starts[d], 128), rows], zparts.at[x, :, rows],
                    z_send, z_recv, to(channel=at_x[d]),
                )

    @pl.when(g == 1)
    def _():
        for d in (1, 2, 3, 0):
            rows = pl.ds(starts[d], 128)
            took(other.at[pl.ds(0, 128)], n_recv.at[d])
            part = lax.dot_general(other[rows, :], half[...], LAST, preferred_element_type=F32)
            zsum[rows, :] = part.astype(BF16)
            if d:
                send(zsum.at[rows], zparts.at[x], z_send, z_recv, to(channel=at_x[d]))

    took(zparts.at[pl.ds(0, 3)], z_recv)
    total = zsum[pl.ds(starts[0], 128), :].astype(F32)
    for d in range(1, 4):
        total = total + zparts[mod4(x + d)].astype(F32)
    zrows[...] = total
    ysend[...] = total.astype(BF16).reshape(4, 32, N)
    for d in range(1, 4):
        send(ysend.at[mod4(yh + d)], yrecv.at[yh], f_send, f_recv, to(channel=at_y[d]))
    took(yrecv.at[pl.ds(0, 3)], f_recv)
    result = zrows[pl.ds(pl.multiple_of(yh * 32, 32), 32), :]
    for d in range(1, 4):
        result = result + yrecv[mod4(yh + d)].astype(F32)
    new_psi_ref[...] = result.astype(BF16)

    out.wait()
    took(gath.at[0 : NCH, 0 : 3], x_send)
    took(gath.at[0 : NCH, 0 : 8], y_send)
    took(gath.at[0 : NCH, 0 : 4], r_send)
    took(near, near_send)
    took(sent.at[0 : NCH, 0 : 14], p_send)
    took(mine, n_send)
    took(zparts.at[pl.ds(0, 3)], z_send)
    took(ysend.at[pl.ds(0, 3)], f_send)


def per_device(env, site_tensor, mpo, channel_mask, block_mask, state_charge, psi):
    dma = pltpu.SemaphoreType.DMA
    hbm = pl.BlockSpec(memory_space=pl.ANY)
    vmem = pl.BlockSpec(memory_space=pltpu.VMEM)
    smem = pl.BlockSpec(memory_space=pltpu.SMEM)
    new_env, new_psi = pl.pallas_call(
        kernel,
        out_shape=(jax.ShapeDtypeStruct((N, N), BF16), jax.ShapeDtypeStruct((32, N), BF16)),
        in_specs=[smem, smem, hbm, hbm, vmem, vmem, hbm],
        out_specs=(hbm, vmem),
        scratch_shapes=[
            pltpu.VMEM((4, N, N), BF16),
            pltpu.VMEM((4, N, N), BF16),
            pltpu.VMEM((2, N, N), BF16),
            pltpu.VMEM((N, N), BF16),
            pltpu.VMEM((N, N), BF16),
            pltpu.VMEM((256, 256), BF16),
            pltpu.VMEM((NCH, 16, R, N), BF16),
            pltpu.VMEM((16, R, N), BF16),
            pltpu.VMEM((NCH, 16, R, N), BF16),
            pltpu.VMEM((NCH, 16, R, N), BF16),
            pltpu.VMEM((NCH, N, 16 * R), BF16),
            pltpu.VMEM((N, N), F32),
            pltpu.VMEM((N, N), BF16),
            pltpu.VMEM((N, N), BF16),
            pltpu.VMEM((N, N), BF16),
            pltpu.VMEM((N, N), BF16),
            pltpu.VMEM((4, 128, N), BF16),
            pltpu.VMEM((128, N), F32),
            pltpu.VMEM((4, 32, N), BF16),
            pltpu.VMEM((4, 32, N), BF16),
            dma, dma, dma, dma,
            dma, dma((NCH,)), dma, dma((NCH, 2)), dma, dma((NCH, 2)), dma, dma,
            dma, dma((NCH,)), dma, dma((4,)), dma, dma, dma, dma,
        ],
        compiler_params=pltpu.CompilerParams(
            collective_id=0, has_side_effects=True, vmem_limit_bytes=40 * 1024 * 1024
        ),
    )(
        state_charge,
        block_mask.reshape(4),
        env.reshape(N, N),
        site_tensor.reshape(4, N, N),
        jnp.swapaxes(mpo[0], 1, 2),
        channel_mask[0],
        psi.reshape(N, N),
    )
    return new_env.reshape(1, 1, 1, N, N), new_psi.reshape(32, 1, 1, N)


def solution(mesh):
    return jax.shard_map(
        per_device,
        mesh=mesh,
        in_specs=(
            P("section", "channel", "block", None, None),
            P("section", None, "block", None, None),
            P("section", None, None, None),
            P("section", None, None),
            P("section", None, "block"),
            P(),
            P("section", "block", None, None),
        ),
        out_specs=(
            P("section", "channel", "block", None, None),
            P("channel", "section", "block", None),
        ),
        check_vma=False,
    )
```

time: 583 us -> 92.1 us (0.16)
  the two profiles are of different devices: /device:TPU:338 before, /device:TPU:446 now
where the time goes in v1:
time: 92.1 us; the launch traced here: 91.7 us
  Pallas kernels  83.3 us (90%)
  local copies, waits for them, and re-layouts  7.8 us (8%)
    pallas_call x1, Pallas kernels, per_device(): pl.pallas_call(kernel, out_shape=(jax.ShapeDtypeStruct((N, N), BF16), jax...  83.3 us
    unnamed x16, local copies, waits for them, and re-layouts  7.8 us

profile of v1, /device:TPU:446, one launch (start us, length us, event | category | flops | bytes accessed | tf_op | source)
XLA Modules:
  0.0 91.7 jit_solution(4591336053761403613)
XLA Ops:
  0.6 0.0 copy-start
  0.6 1.6 %copy-done = bf16[1,4,1,512,512]{4,3,2,1,0:T(8,128)(2,1)S(1)} copy-done((bf16[1,4,1,512,512]{4,3,2,1,0:T(8,128)(2,1)S(1)}, bf16[1,4,1,512,512]{4,3,2,1,0:T(8,128)(2,1)}, u32[]{:S(2)}) %copy-start) | copy-done | bytes 2097176
  2.2 0.0 copy-start.1
  2.2 1.0 %copy-done.1 = bf16[1,1,1,512,512]{4,3,2,1,0:T(8,128)(2,1)S(1)} copy-done((bf16[1,1,1,512,512]{4,3,2,1,0:T(8,128)(2,1)S(1)}, bf16[1,1,1,512,512]{4,3,2,1,0:T(8,128)(2,1)}, u32[]{:S(2)}) %copy-start.1) | copy-done | bytes 524312
  3.3 0.0 copy-start.2
  3.3 1.0 %copy-done.2 = bf16[1,1,512,512]{3,2,1,0:T(8,128)(2,1)S(1)} copy-done((bf16[1,1,512,512]{3,2,1,0:T(8,128)(2,1)S(1)}, bf16[1,1,512,512]{3,2,1,0:T(8,128)(2,1)}, u32[]{:S(2)}) %copy-start.2) | copy-done | bytes 524312
  4.3 0.0 copy-start.3
  4.3 0.7 copy-done.3
  5.0 0.0 copy-start.4
  5.0 0.7 copy-done.4
  5.7 0.0 copy-start.5
  5.7 0.7 copy-done.5
  6.4 0.0 copy-start.6
  6.4 0.7 copy-done.6
  7.0 83.3 %shard_map.86 = (bf16[512,512]{1,0:T(8,128)(2,1)S(1)}, bf16[32,512]{1,0:T(8,128)(2,1)S(1)}) custom-call(s32[4]{0:T(128)S(1)} %copy-done.5, s32[4]{0:T(128)S(1)} %bitcast.17, bf16[512,512]{1,0:T(8,128)(2,1)S(1)} %bitcast.12, bf16[4,512,512]{2,1,0:T(8,128)(2,1)S(1)} %bitcast.10, bf16[16,4,16]{2,1,0:T(4,128)(2,1)S(1)} %bitcast.15, s32[16,16]{1,0:T(8,128)S(1)} %bitcast.16, ...), custom_call_target="tpu_custom_call" | custom-call | tf_op jit(solution)/shard_map/pallas_call | solution.py:295
  90.3 0.8 copy.11
  91.1 0.6 copy.12
Async XLA Ops:
  0.6 1.6 %copy-start = (bf16[1,4,1,512,512]{4,3,2,1,0:T(8,128)(2,1)S(1)}, bf16[1,4,1,512,512]{4,3,2,1,0:T(8,128)(2,1)}, u32[]{:S(2)}) copy-start(bf16[1,4,1,512,512]{4,3,2,1,0:T(8,128)(2,1)} %param.8) | copy-start | bytes 6291460
  2.2 1.0 %copy-start.1 = (bf16[1,1,1,512,512]{4,3,2,1,0:T(8,128)(2,1)S(1)}, bf16[1,1,1,512,512]{4,3,2,1,0:T(8,128)(2,1)}, u32[]{:S(2)}) copy-start(bf16[1,1,1,512,512]{4,3,2,1,0:T(8,128)(2,1)} %param.7) | copy-start | bytes 1572868
  3.3 1.0 %copy-start.2 = (bf16[1,1,512,512]{3,2,1,0:T(8,128)(2,1)S(1)}, bf16[1,1,512,512]{3,2,1,0:T(8,128)(2,1)}, u32[]{:S(2)}) copy-start(bf16[1,1,512,512]{3,2,1,0:T(8,128)(2,1)} %param.13) | copy-start | bytes 1572868
  4.3 0.7 copy-start.3
  5.0 0.7 copy-start.4
  5.7 0.7 copy-start.5
  6.4 0.7 copy-start.6

commit v2 on v1

v2 whole, which is shorter than its diff:
```python
import functools

import jax
import jax.numpy as jnp
from jax import lax
from jax.experimental import pallas as pl
from jax.experimental.pallas import tpu as pltpu
from jax.sharding import PartitionSpec as P

MESH = pl.DeviceIdType.MESH
F32, BF16 = jnp.float32, jnp.bfloat16
N = 512
BLOCKS = 8
CHUNKS = ((0, 1), (1, 1), (2, 1), (3, 1), (4, 1), (5, 1), (6, 1), (7, 1))
SWAPS = ((0, 1), (1, 1), (2, 6))
NCH = len(CHUNKS)
WIDEST = max(n for _, n in CHUNKS)
LAG = 4
LAST = (((1,), (1,)), ((), ()))


def mod4(value):
    return lax.rem(value, 4)


def mix_matrix(mpo_ref, cmask_ref, bmask_ref, charge_ref, yh):
    rows = lax.broadcasted_iota(jnp.int32, (256, 16), 0)
    lane = lax.broadcasted_iota(jnp.int32, (256, 16), 1)
    want_v = lax.rem(rows // 16, 4) * 4 + yh
    pick_v = (lane == want_v).astype(F32)
    rows_s = lax.broadcasted_iota(jnp.int32, (256, 4), 0)
    lane_s = lax.broadcasted_iota(jnp.int32, (256, 4), 1)
    slots, _ = state_slots(charge_ref)
    pick_s = jnp.zeros((256, 4), F32)
    for s in range(4):
        hit = (lane_s == s) & (rows_s // 64 == slots[s])
        pick_s = jnp.where(hit, bmask_ref[s].astype(F32), pick_s)
    pick_s = pick_s.astype(BF16)
    cmask = cmask_ref[...].astype(F32).astype(BF16)
    allowed = lax.dot_general(pick_v.astype(BF16), cmask, LAST, preferred_element_type=F32)
    values = jnp.zeros((256, 16), F32)
    for w in range(16):
        coupling = jnp.dot(pick_s, mpo_ref[w], preferred_element_type=F32) * pick_v
        column = jnp.sum(coupling, axis=1, keepdims=True)
        values = jnp.where(lane == w, column, values)
    values = values * allowed
    spread_w = lax.broadcasted_iota(jnp.int32, (16, 256), 0)
    spread_c = lax.broadcasted_iota(jnp.int32, (16, 256), 1) // 16
    spread = (spread_w == lax.rem(spread_c, 4) * 4 + spread_c // 4).astype(BF16)
    full = jnp.dot(values.astype(BF16), spread, preferred_element_type=F32)
    row = lax.broadcasted_iota(jnp.int32, (256, 256), 0)
    col = lax.broadcasted_iota(jnp.int32, (256, 256), 1)
    return jnp.where(lax.rem(row, 16) == lax.rem(col, 16), full, 0.0).astype(BF16)


def state_slots(charge_ref):
    charge = [charge_ref[s] for s in range(4)]
    slots = []
    ones = jnp.int32(0)
    for s in range(4):
        slots.append(jnp.where(charge[s] == 1, 2 + ones, s - ones))
        ones = ones + charge[s]
    order = []
    for k in range(4):
        place = jnp.int32(0)
        for s in range(4):
            place = place + jnp.where(slots[s] == k, s, 0)
        order.append(place)
    return slots, order


def kernel(
    charge_in, bmask_in, env_ref, site_ref, mpo_in, cmask_in, psi_ref,
    new_env_ref, new_psi_ref,
    charge_ref, bmask_ref, mpo_ref, cmask_ref,
    site_v, srt, near, psi_v, psi_t, kmat, gath, mixed, sent, prod, turned, acc,
    other, half, wide, wide_in, summed, kept, ysend, yrecv,
    small_sem, site_sem, psi_sem, own_sem,
    x_send, x_recv, y_send, y_recv, w_recv, r_send, r_recv, near_send, near_recv,
    p_send, p_recv, n_send, n_recv, z_send, z_recv, f_send, f_recv,
):
    g = lax.axis_index("section")
    c = lax.axis_index("channel")
    q = lax.axis_index("block")
    x, yh = c // 4, lax.rem(c, 4)
    up = lax.rem(q + 1, 16)
    down = lax.rem(q + 15, 16)
    target = jnp.where(g == 0, up, down)
    origin = jnp.where(g == 0, down, up)
    fed = jnp.where(g == 0, q > 0, q < 15)
    at_x = [mod4(x + i) * 4 + yh for i in range(4)]
    at_y = [x * 4 + mod4(yh + i) for i in range(4)]
    spans = [pl.ds(first, count) for first, count in CHUNKS]

    def to(channel=None, block=None, section=None):
        where = {}
        if section is not None:
            where["section"] = section
        if channel is not None:
            where["channel"] = channel
        if block is not None:
            where["block"] = block
        return where

    def send(src, dst, send_sem, recv_sem, where):
        pltpu.make_async_remote_copy(
            src_ref=src, dst_ref=dst, send_sem=send_sem, recv_sem=recv_sem, device_id=where, device_id_type=MESH
        ).start()

    def took(ref, sem):
        pltpu.make_async_copy(ref, ref, sem).wait()

    small = [
        pltpu.make_async_copy(charge_in, charge_ref, small_sem.at[0]),
        pltpu.make_async_copy(bmask_in, bmask_ref, small_sem.at[1]),
        pltpu.make_async_copy(mpo_in, mpo_ref, small_sem.at[2]),
        pltpu.make_async_copy(cmask_in, cmask_ref, small_sem.at[3]),
    ]
    for copy in small:
        copy.start()
    own_in = pltpu.make_async_copy(env_ref.at[pl.ds(x * BLOCKS, BLOCKS)], gath.at[:, yh * 4 + x], own_sem)
    own_in.start()
    site_in = pltpu.make_async_copy(site_ref, site_v, site_sem)
    site_in.start()
    psi_in = pltpu.make_async_copy(psi_ref, psi_v, psi_sem)
    psi_in.start()

    barrier = pltpu.get_barrier_semaphore()
    for i in range(1, 4):
        pl.semaphore_signal(barrier, inc=1, device_id=to(channel=at_x[i]), device_id_type=MESH)
        pl.semaphore_signal(barrier, inc=1, device_id=to(channel=at_y[i]), device_id_type=MESH)
    for i in range(4):
        pl.semaphore_signal(barrier, inc=1, device_id=to(channel=at_x[i], block=origin), device_id_type=MESH)
    pl.semaphore_signal(barrier, inc=1, device_id=to(section=1 - g), device_id_type=MESH)
    pl.semaphore_wait(barrier, 11)

    for j, (first, count) in enumerate(SWAPS):
        for i in range(1, 4):
            send(
                env_ref.at[pl.ds(mod4(x + i) * BLOCKS + first, count)], gath.at[pl.ds(first, count), yh * 4 + x],
                x_send, x_recv.at[j], to(channel=at_x[i]),
            )

    def pass_on(j):
        if j < len(SWAPS):
            took(gath.at[pl.ds(*SWAPS[j]), pl.ds(0, 3)], x_recv.at[j])
        early = gath.at[spans[j], pl.ds(yh * 4, 2)]
        late = gath.at[spans[j], pl.ds(yh * 4 + 2, 2)]
        send(early, early, y_send, y_recv.at[j, 0], to(channel=at_y[1]))
        send(late, late, y_send, y_recv.at[j, 1], to(channel=at_y[3]))
        send(late, late, y_send, w_recv.at[j, 0], to(channel=at_y[1]))
        send(early, early, y_send, w_recv.at[j, 1], to(channel=at_y[3]))

    def relay(j):
        two = gath.at[spans[j], pl.ds(0, 2)]
        before = gath.at[spans[j], pl.ds(mod4(yh + 3) * 4, 2)]
        took(two, y_recv.at[j, 0])
        send(before, before, r_send, r_recv.at[j, 0], to(channel=at_y[1]))
        after = gath.at[spans[j], pl.ds(mod4(yh + 1) * 4 + 2, 2)]
        took(two, y_recv.at[j, 1])
        send(after, after, r_send, r_recv.at[j, 1], to(channel=at_y[3]))

    def multiply(j):
        first, count = CHUNKS[j]
        for way in range(2):
            took(gath.at[spans[j], pl.ds(0, 2)], w_recv.at[j, way])
            took(gath.at[spans[j], pl.ds(0, 2)], r_recv.at[j, way])
        for i in range(count):
            blended = jnp.dot(kmat[...], gath[first + i].reshape(256, N), preferred_element_type=F32)
            mixed[:, i] = blended.astype(BF16).reshape(4, 4, 16, N)
        for k in range(4):
            product = jnp.dot(mixed[k, 0:count].reshape(count * 64, N), srt[k], preferred_element_type=F32)
            product = product.astype(BF16).reshape(count, 4, 16, N)
            for vx in range(4):
                sent[first : first + count, vx * 4 + k] = product[:, vx]
        for i in range(1, 4):
            v = mod4(x + i)
            send(
                sent.at[spans[j], pl.ds(v * 4, 2)], prod.at[spans[j], pl.ds(x * 4, 2)],
                p_send, p_recv.at[j], to(channel=at_x[i]),
            )
        for i in range(4):
            v = mod4(x + i)
            send(
                sent.at[spans[j], pl.ds(v * 4 + 2, 2)], prod.at[spans[j], pl.ds(x * 4 + 2, 2)],
                p_send, p_recv.at[j], to(channel=at_x[i], block=target),
            )
        prod[first : first + count, pl.ds(x * 4, 2)] = sent[first : first + count, pl.ds(x * 4, 2)]

    def turn(j):
        first, count = CHUNKS[j]
        for b in range(first, first + count):
            pieces = []
            for xs in range(4):
                rows = slice(xs * 128 + b * 16, xs * 128 + b * 16 + 16)
                pieces += [srt[0, rows, :], srt[1, rows, :], near[0, rows, :], near[1, rows, :]]
            turned[b] = jnp.concatenate(pieces, axis=0).T.reshape(4, 4, 32, 256)

    def gained(j, tile):
        first, count = CHUNKS[j]
        part = jnp.zeros((128, N), F32)
        for b in range(first, first + count):
            left = turned[(b, *tile)].reshape(128, 256)
            part = part + jnp.dot(left, prod[b].reshape(256, N), preferred_element_type=F32)
        return part.reshape(4, 32, N)

    def accumulate(j):
        took(prod.at[spans[j], pl.ds(0, 14)], p_recv.at[j])

        def add(t, carry):
            part = gained(j, (t,))
            acc[t] = part if j == 0 else acc[t] + part
            return carry

        lax.fori_loop(0, 4, add, 0)

    def advance(tile, recv_sem):
        new_env_ref[tile] = (acc[tile] + gained(NCH - 1, tile)).astype(BF16)
        send(new_env_ref.at[tile], other.at[tile], n_send, recv_sem, to(section=1 - g))

    for copy in small:
        copy.wait()
    own_in.wait()
    pass_on(0)
    site_in.wait()
    _, order = state_slots(charge_ref)
    for k in (2, 3, 0, 1):
        srt[k] = site_v[order[k]]
        if k == 3:
            send(srt.at[pl.ds(2, 2)], near, near_send, near_recv, to(block=target))
    pass_on(1)
    kmat[...] = mix_matrix(mpo_ref, cmask_ref, bmask_ref, charge_ref, yh)

    for j in range(NCH):
        relay(j)
        if j + 2 < NCH:
            pass_on(j + 2)
        if j == 1:
            psi_in.wait()

            @pl.when(g == 0)
            def _():
                psi_t[...] = psi_v[...]

            @pl.when(g == 1)
            def _():
                psi_t[...] = psi_v[...].T

        if j == LAG - 1:
            took(near, near_recv)

            @pl.when(jnp.logical_not(fed))
            def _():
                near[...] = jnp.zeros_like(near)

        if j >= LAG:
            accumulate(j - LAG)
        if j >= 1:
            multiply(j - 1)
        if j >= LAG - 1:
            turn(j - LAG + 1)
    multiply(NCH - 1)
    for j in range(NCH - LAG + 1, NCH):
        turn(j)
    for j in range(NCH - LAG, NCH - 1):
        accumulate(j)

    took(prod.at[spans[-1], pl.ds(0, 14)], p_recv.at[NCH - 1])
    all_rows = slice(None)
    hand = [mod4(yh + d) for d in range(4)]

    @pl.when(g == 0)
    def _():
        for d in (1, 2, 3, 0):
            advance((all_rows, hand[d]), n_recv.at[d])

    @pl.when(g == 1)
    def _():
        for t in range(4):
            advance((t,), n_recv.at[t])

    for t in range(4):
        rows = new_env_ref[t].reshape(128, N)
        half[t] = jnp.dot(rows, psi_t[...], preferred_element_type=F32).astype(BF16).reshape(4, 32, N)
    quarter = other.at[0]

    @pl.when(g == 0)
    def _():
        def settle(t):
            columns = slice(t * 128, t * 128 + 128)
            took(wide_in.at[pl.ds(0, 3), :, :, columns], z_recv.at[t])
            total = wide[x, :, :, columns].astype(F32)
            for d in range(1, 4):
                total = total + wide_in[mod4(x + d), :, :, columns].astype(F32)
            summed[:, :, columns] = total
            ysend[:, :, columns] = total.astype(BF16)
            for d in range(1, 4):
                send(
                    ysend.at[hand[d], :, columns], yrecv.at[yh, :, columns],
                    f_send, f_recv, to(channel=at_y[d]),
                )

        for t in range(4):
            columns = slice(t * 128, t * 128 + 128)
            took(quarter, n_recv.at[t])
            part = lax.dot_general(half[...].reshape(N, N), other[t].reshape(128, N), LAST, preferred_element_type=F32)
            wide[:, :, :, columns] = part.astype(BF16).reshape(4, 4, 32, 128)
            for d in range(1, 4):
                send(
                    wide.at[mod4(x + d), :, :, columns], wide_in.at[x, :, :, columns],
                    z_send, z_recv.at[t], to(channel=at_x[d]),
                )
            if t:
                settle(t - 1)
        settle(3)
        kept[...] = summed[yh]

    @pl.when(g == 1)
    def _():
        def settle(d):
            took(wide_in.at[d, pl.ds(0, 3)], z_recv.at[d])
            total = wide[d, x].astype(F32)
            for e in range(1, 4):
                total = total + wide_in[d, mod4(x + e)].astype(F32)
            if d:
                ysend[d] = total.astype(BF16)
                send(ysend.at[d], yrecv.at[yh], f_send, f_recv, to(channel=at_y[d]))
            else:
                kept[...] = total

        for d in (1, 2, 3, 0):
            took(quarter, n_recv.at[d])
            rows = other[:, hand[d]].reshape(128, N)
            part = lax.dot_general(rows, half[...].reshape(N, N), LAST, preferred_element_type=F32)
            wide[d] = part.astype(BF16).reshape(4, 32, N)
            for e in range(1, 4):
                send(wide.at[d, mod4(x + e)], wide_in.at[d, x], z_send, z_recv.at[d], to(channel=at_x[e]))
            if d != 1:
                settle((d + 3) % 4)
        settle(0)

    took(gath.at[:, 0:3], x_send)
    took(gath.at[:, 0:8], y_send)
    took(gath.at[:, 0:4], r_send)
    took(near, near_send)
    took(sent.at[:, 0:14], p_send)
    took(new_env_ref, n_send)
    took(wide_in.at[pl.ds(0, 3)], z_send)
    took(yrecv.at[pl.ds(0, 3)], f_recv)
    result = kept[...]
    for d in range(1, 4):
        result = result + yrecv[mod4(yh + d)].astype(F32)
    new_psi_ref[...] = result.astype(BF16)
    took(ysend.at[pl.ds(0, 3)], f_send)


def per_device(env, site_tensor, mpo, channel_mask, block_mask, state_charge, psi):
    dma = pltpu.SemaphoreType.DMA
    hbm = pl.BlockSpec(memory_space=pltpu.HBM)
    vmem = pl.BlockSpec(memory_space=pltpu.VMEM)
    new_env, new_psi = pl.pallas_call(
        kernel,
        out_shape=(pltpu.VMEM((4, 4, 32, N), BF16), pltpu.VMEM((32, N), BF16)),
        in_specs=[hbm] * 7,
        out_specs=(vmem, vmem),
        scratch_shapes=[
            pltpu.SMEM((4,), jnp.int32),
            pltpu.SMEM((4,), jnp.int32),
            pltpu.VMEM((16, 4, 16), BF16),
            pltpu.VMEM((16, 16), jnp.int32),
            pltpu.VMEM((4, N, N), BF16),
            pltpu.VMEM((4, N, N), BF16),
            pltpu.VMEM((2, N, N), BF16),
            pltpu.VMEM((N, N), BF16),
            pltpu.VMEM((N, N), BF16),
            pltpu.VMEM((256, 256), BF16),
            pltpu.VMEM((BLOCKS, 16, 16, N), BF16),
            pltpu.VMEM((4, WIDEST, 4, 16, N), BF16),
            pltpu.VMEM((BLOCKS, 16, 16, N), BF16),
            pltpu.VMEM((BLOCKS, 16, 16, N), BF16),
            pltpu.VMEM((BLOCKS, 4, 4, 32, 256), BF16),
            pltpu.VMEM((4, 4, 32, N), F32),
            pltpu.VMEM((4, 4, 32, N), BF16),
            pltpu.VMEM((4, 4, 32, N), BF16),
            pltpu.VMEM((4, 4, 32, N), BF16),
            pltpu.VMEM((4, 4, 32, N), BF16),
            pltpu.VMEM((4, 32, N), F32),
            pltpu.VMEM((32, N), F32),
            pltpu.VMEM((4, 32, N), BF16),
            pltpu.VMEM((4, 32, N), BF16),
            dma((4,)), dma, dma, dma,
            dma, dma((len(SWAPS),)), dma, dma((NCH, 2)), dma((NCH, 2)), dma, dma((NCH, 2)), dma, dma,
            dma, dma((NCH,)), dma, dma((4,)), dma, dma((4,)), dma, dma,
        ],
        compiler_params=pltpu.CompilerParams(
            collective_id=0, has_side_effects=True, vmem_limit_bytes=56 * 1024 * 1024
        ),
    )(
        *[
            pltpu.with_memory_space_constraint(a, pltpu.HBM)
            for a in (
                state_charge,
                block_mask.reshape(4),
                env.reshape(4 * BLOCKS, 16, N),
                site_tensor.reshape(4, N, N),
                jnp.swapaxes(mpo[0], 1, 2),
                channel_mask[0],
                psi.reshape(N, N),
            )
        ]
    )
    return new_env.reshape(1, 1, 1, N, N), new_psi.reshape(32, 1, 1, N)


def solution(mesh):
    return jax.shard_map(
        per_device,
        mesh=mesh,
        in_specs=(
            P("section", "channel", "block", None, None),
            P("section", None, "block", None, None),
            P("section", None, None, None),
            P("section", None, None),
            P("section", None, "block"),
            P(),
            P("section", "block", None, None),
        ),
        out_specs=(
            P("section", "channel", "block", None, None),
            P("channel", "section", "block", None),
        ),
        check_vma=False,
    )
```

time: 92.1 us -> 81.7 us (0.89)
  the two profiles are of different devices: /device:TPU:446 before, /device:TPU:16 now
where the time goes in v2:
time: 81.7 us; the launch traced here: 81.5 us
  Pallas kernels  79.5 us (97%)
  local copies, waits for them, and re-layouts  1.41 us (2%)
    pallas_call x1, Pallas kernels, per_device(): pl.pallas_call(kernel, out_shape=(pltpu.VMEM((4, 4, 32, N), BF16), pltpu....  79.5 us

profile of v2, /device:TPU:16, one launch (start us, length us, event | category | flops | bytes accessed | tf_op | source)
XLA Modules:
  0.0 81.5 jit_solution(9999481123173716216)
XLA Ops:
  0.6 79.5 %shard_map.86 = (bf16[4,4,32,512]{3,2,1,0:T(8,128)(2,1)S(1)}, bf16[32,512]{1,0:T(8,128)(2,1)S(1)}) custom-call(s32[4]{0:T(128)} %charge_in.1, s32[4]{0:T(128)} %bitcast.17, bf16[32,16,512]{2,1,0:T(8,128)(2,1)} %bitcast.13, bf16[4,512,512]{2,1,0:T(8,128)(2,1)} %bitcast.12, bf16[16,4,16]{2,1,0:T(4,128)(2,1)} %bitcast.15, s32[16,16]{1,0:T(8,128)} %bitcast.16, ...), custom_call_target="tpu_custom_call" | custom-call | tf_op jit(solution)/shard_map/pallas_call | solution.py:361
  80.1 0.8 copy.11
  80.9 0.6 copy.12

commit v3 on v2

--- a/solution.py
+++ b/solution.py
@@ -12,10 +12,12 @@
 N = 512
 BLOCKS = 8
 CHUNKS = ((0, 1), (1, 1), (2, 1), (3, 1), (4, 1), (5, 1), (6, 1), (7, 1))
-SWAPS = ((0, 1), (1, 1), (2, 6))
 NCH = len(CHUNKS)
 WIDEST = max(n for _, n in CHUNKS)
 LAG = 4
+OWN_FIRST = 0
+AHEAD = 2
+LOOK = 2
 LAST = (((1,), (1,)), ((), ()))
 
 
@@ -76,7 +78,7 @@
     site_v, srt, near, psi_v, psi_t, kmat, gath, mixed, sent, prod, turned, acc,
     other, half, wide, wide_in, summed, kept, ysend, yrecv,
     small_sem, site_sem, psi_sem, own_sem,
-    x_send, x_recv, y_send, y_recv, w_recv, r_send, r_recv, near_send, near_recv,
+    x_send, x_recv, y_send, y_recv, r_send, r_recv, near_send, near_recv,
     p_send, p_recv, n_send, n_recv, z_send, z_recv, f_send, f_recv,
 ):
     g = lax.axis_index("section")
@@ -88,6 +90,7 @@
     target = jnp.where(g == 0, up, down)
     origin = jnp.where(g == 0, down, up)
     fed = jnp.where(g == 0, q > 0, q < 15)
+    feeds = jnp.where(g == 0, q < 15, q > 0)
     at_x = [mod4(x + i) * 4 + yh for i in range(4)]
     at_y = [x * 4 + mod4(yh + i) for i in range(4)]
     spans = [pl.ds(first, count) for first, count in CHUNKS]
@@ -129,41 +132,64 @@
     for i in range(1, 4):
         pl.semaphore_signal(barrier, inc=1, device_id=to(channel=at_x[i]), device_id_type=MESH)
         pl.semaphore_signal(barrier, inc=1, device_id=to(channel=at_y[i]), device_id_type=MESH)
-    for i in range(4):
-        pl.semaphore_signal(barrier, inc=1, device_id=to(channel=at_x[i], block=origin), device_id_type=MESH)
     pl.semaphore_signal(barrier, inc=1, device_id=to(section=1 - g), device_id_type=MESH)
-    pl.semaphore_wait(barrier, 11)
-
-    for j, (first, count) in enumerate(SWAPS):
+
+    @pl.when(fed)
+    def _():
+        for i in range(4):
+            pl.semaphore_signal(barrier, inc=1, device_id=to(channel=at_x[i], block=origin), device_id_type=MESH)
+
+    pl.semaphore_wait(barrier, jnp.where(feeds, 11, 7))
+
+    def pass_own(j):
+        first, count = CHUNKS[j]
+        mine = env_ref.at[pl.ds(x * BLOCKS + first, count)]
+        there = gath.at[spans[j], yh * 4 + x]
+        send(mine, there, y_send, y_recv.at[j, 0], to(channel=at_y[1]))
+        send(mine, there, y_send, y_recv.at[j, 1], to(channel=at_y[3]))
+
+    def swap(j):
+        if j >= NCH:
+            return
+        first, count = CHUNKS[j]
         for i in range(1, 4):
             send(
-                env_ref.at[pl.ds(mod4(x + i) * BLOCKS + first, count)], gath.at[pl.ds(first, count), yh * 4 + x],
+                env_ref.at[pl.ds(mod4(x + i) * BLOCKS + first, count)], gath.at[spans[j], yh * 4 + x],
                 x_send, x_recv.at[j], to(channel=at_x[i]),
             )
+        if j < OWN_FIRST:
+            pass_own(j)
+
+    for j in range(AHEAD):
+        swap(j)
 
     def pass_on(j):
-        if j < len(SWAPS):
-            took(gath.at[pl.ds(*SWAPS[j]), pl.ds(0, 3)], x_recv.at[j])
-        early = gath.at[spans[j], pl.ds(yh * 4, 2)]
-        late = gath.at[spans[j], pl.ds(yh * 4 + 2, 2)]
-        send(early, early, y_send, y_recv.at[j, 0], to(channel=at_y[1]))
-        send(late, late, y_send, y_recv.at[j, 1], to(channel=at_y[3]))
-        send(late, late, y_send, w_recv.at[j, 0], to(channel=at_y[1]))
-        send(early, early, y_send, w_recv.at[j, 1], to(channel=at_y[3]))
+        if j >= NCH:
+            return
+        took(gath.at[spans[j], pl.ds(0, 3)], x_recv.at[j])
+        if j < OWN_FIRST:
+            beside = x + 1 - 2 * lax.rem(x, 2)
+            apart = 2 - 2 * (x // 2)
+            parts = [gath.at[spans[j], pl.ds(yh * 4 + apart, 2)], gath.at[spans[j], yh * 4 + beside]]
+        else:
+            parts = [gath.at[spans[j], pl.ds(yh * 4, 4)]]
+        for rows in parts:
+            send(rows, rows, y_send, y_recv.at[j, 0], to(channel=at_y[1]))
+            send(rows, rows, y_send, y_recv.at[j, 1], to(channel=at_y[3]))
+        swap(j + AHEAD)
 
     def relay(j):
-        two = gath.at[spans[j], pl.ds(0, 2)]
+        four = gath.at[spans[j], pl.ds(0, 4)]
         before = gath.at[spans[j], pl.ds(mod4(yh + 3) * 4, 2)]
-        took(two, y_recv.at[j, 0])
+        took(four, y_recv.at[j, 0])
         send(before, before, r_send, r_recv.at[j, 0], to(channel=at_y[1]))
         after = gath.at[spans[j], pl.ds(mod4(yh + 1) * 4 + 2, 2)]
-        took(two, y_recv.at[j, 1])
+        took(four, y_recv.at[j, 1])
         send(after, after, r_send, r_recv.at[j, 1], to(channel=at_y[3]))
 
     def multiply(j):
         first, count = CHUNKS[j]
         for way in range(2):
-            took(gath.at[spans[j], pl.ds(0, 2)], w_recv.at[j, way])
             took(gath.at[spans[j], pl.ds(0, 2)], r_recv.at[j, way])
         for i in range(count):
             blended = jnp.dot(kmat[...], gath[first + i].reshape(256, N), preferred_element_type=F32)
@@ -179,12 +205,16 @@
                 sent.at[spans[j], pl.ds(v * 4, 2)], prod.at[spans[j], pl.ds(x * 4, 2)],
                 p_send, p_recv.at[j], to(channel=at_x[i]),
             )
-        for i in range(4):
-            v = mod4(x + i)
-            send(
-                sent.at[spans[j], pl.ds(v * 4 + 2, 2)], prod.at[spans[j], pl.ds(x * 4 + 2, 2)],
-                p_send, p_recv.at[j], to(channel=at_x[i], block=target),
-            )
+
+        @pl.when(feeds)
+        def _():
+            for i in range(4):
+                v = mod4(x + i)
+                send(
+                    sent.at[spans[j], pl.ds(v * 4 + 2, 2)], prod.at[spans[j], pl.ds(x * 4 + 2, 2)],
+                    p_send, p_recv.at[j], to(channel=at_x[i], block=target),
+                )
+
         prod[first : first + count, pl.ds(x * 4, 2)] = sent[first : first + count, pl.ds(x * 4, 2)]
 
     def turn(j):
@@ -204,8 +234,17 @@
             part = part + jnp.dot(left, prod[b].reshape(256, N), preferred_element_type=F32)
         return part.reshape(4, 32, N)
 
+    def receive(j):
+        @pl.when(fed)
+        def _():
+            took(prod.at[spans[j], pl.ds(0, 14)], p_recv.at[j])
+
+        @pl.when(jnp.logical_not(fed))
+        def _():
+            took(prod.at[spans[j], pl.ds(0, 6)], p_recv.at[j])
+
     def accumulate(j):
-        took(prod.at[spans[j], pl.ds(0, 14)], p_recv.at[j])
+        receive(j)
 
         def add(t, carry):
             part = gained(j, (t,))
@@ -227,14 +266,18 @@
     for k in (2, 3, 0, 1):
         srt[k] = site_v[order[k]]
         if k == 3:
-            send(srt.at[pl.ds(2, 2)], near, near_send, near_recv, to(block=target))
-    pass_on(1)
+
+            @pl.when(feeds)
+            def _():
+                send(srt.at[pl.ds(2, 2)], near, near_send, near_recv, to(block=target))
+
+    for j in range(1, LOOK):
+        pass_on(j)
     kmat[...] = mix_matrix(mpo_ref, cmask_ref, bmask_ref, charge_ref, yh)
 
     for j in range(NCH):
         relay(j)
-        if j + 2 < NCH:
-            pass_on(j + 2)
+        pass_on(j + LOOK)
         if j == 1:
             psi_in.wait()
 
@@ -247,25 +290,29 @@
                 psi_t[...] = psi_v[...].T
 
         if j == LAG - 1:
-            took(near, near_recv)
+            @pl.when(fed)
+            def _():
+                took(near, near_recv)
 
             @pl.when(jnp.logical_not(fed))
             def _():
                 near[...] = jnp.zeros_like(near)
+                for xs in range(4):
+                    prod[:, xs * 4 + 2 : xs * 4 + 4] = jnp.zeros((BLOCKS, 2, 16, N), BF16)
 
         if j >= LAG:
             accumulate(j - LAG)
         if j >= 1:
             multiply(j - 1)
-        if j >= LAG - 1:
-            turn(j - LAG + 1)
+        for b in (2 * (j - LAG + 1), 2 * (j - LAG + 1) + 1):
+            if 0 <= b < NCH:
+                turn(b)
+    accumulate(NCH - LAG)
     multiply(NCH - 1)
-    for j in range(NCH - LAG + 1, NCH):
-        turn(j)
-    for j in range(NCH - LAG, NCH - 1):
+    for j in range(NCH - LAG + 1, NCH - 1):
         accumulate(j)
 
-    took(prod.at[spans[-1], pl.ds(0, 14)], p_recv.at[NCH - 1])
+    receive(NCH - 1)
     all_rows = slice(None)
     hand = [mod4(yh + d) for d in range(4)]
 
@@ -342,8 +389,16 @@
     took(gath.at[:, 0:3], x_send)
     took(gath.at[:, 0:8], y_send)
     took(gath.at[:, 0:4], r_send)
-    took(near, near_send)
-    took(sent.at[:, 0:14], p_send)
+
+    @pl.when(feeds)
+    def _():
+        took(near, near_send)
+        took(sent.at[:, 0:14], p_send)
+
+    @pl.when(jnp.logical_not(feeds))
+    def _():
+        took(sent.at[:, 0:6], p_send)
+
     took(new_env_ref, n_send)
     took(wide_in.at[pl.ds(0, 3)], z_send)
     took(yrecv.at[pl.ds(0, 3)], f_recv)
@@ -389,7 +444,7 @@
             pltpu.VMEM((4, 32, N), BF16),
             pltpu.VMEM((4, 32, N), BF16),
             dma((4,)), dma, dma, dma,
-            dma, dma((len(SWAPS),)), dma, dma((NCH, 2)), dma((NCH, 2)), dma, dma((NCH, 2)), dma, dma,
+            dma, dma((NCH,)), dma, dma((NCH, 2)), dma, dma((NCH, 2)), dma, dma,
             dma, dma((NCH,)), dma, dma((4,)), dma, dma((4,)), dma, dma,
         ],
         compiler_params=pltpu.CompilerParams(

time: 81.7 us -> 77.6 us (0.950)
  the two profiles are of different devices: /device:TPU:16 before, /device:TPU:384 now
where the time goes in v3:
time: 77.6 us; the launch traced here: 77.5 us
  Pallas kernels  75.4 us (97%)
  local copies, waits for them, and re-layouts  1.41 us (2%)
    pallas_call x1, Pallas kernels, per_device(): pl.pallas_call(kernel, out_shape=(pltpu.VMEM((4, 4, 32, N), BF16), pltpu....  75.4 us

profile of v3, /device:TPU:384, one launch (start us, length us, event | category | flops | bytes accessed | tf_op | source)
XLA Modules:
  0.0 77.5 jit_solution(14218301047969032385)
XLA Ops:
  0.6 75.4 %shard_map.86 = (bf16[4,4,32,512]{3,2,1,0:T(8,128)(2,1)S(1)}, bf16[32,512]{1,0:T(8,128)(2,1)S(1)}) custom-call(s32[4]{0:T(128)} %charge_in.1, s32[4]{0:T(128)} %bitcast.17, bf16[32,16,512]{2,1,0:T(8,128)(2,1)} %bitcast.13, bf16[4,512,512]{2,1,0:T(8,128)(2,1)} %bitcast.12, bf16[16,4,16]{2,1,0:T(4,128)(2,1)} %bitcast.15, s32[16,16]{1,0:T(8,128)} %bitcast.16, ...), custom_call_target="tpu_custom_call" | custom-call | tf_op jit(solution)/shard_map/pallas_call | solution.py:416
  76.1 0.8 %copy.11 = bf16[1,1,1,512,512]{4,3,2,1,0:T(8,128)(2,1)} copy(bf16[1,1,1,512,512]{4,3,2,1,0:T(8,128)(2,1)S(1)} %bitcast.10) | data formatting | bytes 1048576
  76.9 0.6 copy.12

commit v4 on v3

--- a/solution.py
+++ b/solution.py
@@ -199,7 +199,7 @@
             product = product.astype(BF16).reshape(count, 4, 16, N)
             for vx in range(4):
                 sent[first : first + count, vx * 4 + k] = product[:, vx]
-        for i in range(1, 4):
+        for i in (2, 1, 3):
             v = mod4(x + i)
             send(
                 sent.at[spans[j], pl.ds(v * 4, 2)], prod.at[spans[j], pl.ds(x * 4, 2)],
@@ -208,7 +208,7 @@
 
         @pl.when(feeds)
         def _():
-            for i in range(4):
+            for i in (2, 1, 3, 0):
                 v = mod4(x + i)
                 send(
                     sent.at[spans[j], pl.ds(v * 4 + 2, 2)], prod.at[spans[j], pl.ds(x * 4 + 2, 2)],

time: 77.6 us -> 77.6 us (level)
  the two profiles are of different devices: /device:TPU:384 before, /device:TPU:320 now
where the time goes in v4:
time: 77.6 us; the launch traced here: 77.5 us
  Pallas kernels  75.4 us (97%)
  local copies, waits for them, and re-layouts  1.41 us (2%)
    pallas_call x1, Pallas kernels, per_device(): pl.pallas_call(kernel, out_shape=(pltpu.VMEM((4, 4, 32, N), BF16), pltpu....  75.4 us

profile of v4, /device:TPU:320, one launch (start us, length us, event | category | flops | bytes accessed | tf_op | source)
XLA Modules:
  0.0 77.5 jit_solution(8834186817476310678)
XLA Ops:
  0.6 75.4 %shard_map.86 = (bf16[4,4,32,512]{3,2,1,0:T(8,128)(2,1)S(1)}, bf16[32,512]{1,0:T(8,128)(2,1)S(1)}) custom-call(s32[4]{0:T(128)} %charge_in.1, s32[4]{0:T(128)} %bitcast.17, bf16[32,16,512]{2,1,0:T(8,128)(2,1)} %bitcast.13, bf16[4,512,512]{2,1,0:T(8,128)(2,1)} %bitcast.12, bf16[16,4,16]{2,1,0:T(4,128)(2,1)} %bitcast.15, s32[16,16]{1,0:T(8,128)} %bitcast.16, ...), custom_call_target="tpu_custom_call" | custom-call | tf_op jit(solution)/shard_map/pallas_call | solution.py:416
  76.0 0.8 %copy.11 = bf16[1,1,1,512,512]{4,3,2,1,0:T(8,128)(2,1)} copy(bf16[1,1,1,512,512]{4,3,2,1,0:T(8,128)(2,1)S(1)} %bitcast.10) | data formatting | bytes 1048576
  76.8 0.6 copy.12
